TPU v7x, 256 devices: a whole 4x4x8 slice. The times are simulated.
256 devices in a mesh: dp: 32 (over y, x, core), ind: 8 (over z).
Axes of the slice: x: 4, y: 4, z: 8, core: 2. Of those that a mesh axis runs over, the one named last changes fastest.
Arguments:
- inputs: bfloat16 [65536, 256], P('dp'), may hold values from -6 to 6
- targets: bfloat16 [65536], P('dp'), may hold values from -6 to 6
- row_counts: int32 [32], replicated, may hold values from 1 to 2048, 32768 in all
- w_in: bfloat16 [256, 1024], replicated, may hold values from -0.375 to 0.375
- w_mid: bfloat16 [1024, 1024], replicated, may hold values from -0.1875 to 0.1875
- w_out: bfloat16 [1024, 128], replicated, may hold values from -0.1875 to 0.1875
- feat_gain: float32 [128], replicated, may hold values from 0.1 to 1.9
- inducing: bfloat16 [16384, 128], P('ind'), may hold values from -6 to 6
- log_scale: float32 [1], replicated, may hold values from -0.5 to 0.5
- lengthscale: float32 [1], replicated, may hold values from 3.2 to 3.5
- noise_var: float32 [1], replicated, may hold values from 5e-05 to 0.0002
Outputs:
- panel_factor: float32 [16384, 512], P(('ind', 'dp'))
- rhs_next: float32 [16384], P(('ind', 'dp'))
- panel_solution: float32 [512], replicated
- log_det: float32 [1], replicated
Inputs may be any that keep to these rules, and one draw needn't show every extreme that they name: The first row_counts[s] samples of shard s are valid; the counts sum to 32768 and one shard has all 2048 slots valid.
All inputs are finite; a program needn't handle non-finite values.
Results may differ from a plain program's by a relative error of at most 0.012.
The roundings to bfloat16 on the way count: a program that leaves them out, or rounds other values in their place, can miss the bound.
Values may be sent and summed in bfloat16 or wider, within the bound.
No kernel may reach another device: no remote copies, remote signals or barrier semaphores. Data moves between devices by JAX's collectives and lax.ppermute only.
A program may use at most 64 MiB of HBM per device.

v0:
```python
import jax
import jax.numpy as jnp
from jax import lax
from jax.sharding import PartitionSpec as P

PB = 512
JITTER = 0.0001


def from_root(shard, axis, root):
    mine = lax.axis_index(axis) == root
    return lax.psum(jnp.where(mine, shard, jnp.zeros_like(shard)), axis)


def embed(inputs, w_in, w_mid, w_out, feat_gain):
    hidden_one = jax.nn.gelu(jnp.dot(inputs, w_in, preferred_element_type=jnp.float32)).astype(
        jnp.bfloat16
    )
    hidden_two = jax.nn.gelu(jnp.dot(hidden_one, w_mid, preferred_element_type=jnp.float32)).astype(
        jnp.bfloat16
    )
    projected = jnp.dot(hidden_two, w_out, preferred_element_type=jnp.float32)
    scaled = (
        projected
        * lax.rsqrt(jnp.mean(projected * projected, axis=-1, keepdims=True) + 1e-06)
        * feat_gain
    )
    return scaled.astype(jnp.bfloat16)


def exponent(points, others, scale_log, inverse_sq):
    point_sq = jnp.sum(jnp.square(points.astype(jnp.float32)), axis=1)
    other_sq = jnp.sum(jnp.square(others.astype(jnp.float32)), axis=1)
    cross_term = jnp.dot(points, others.T, preferred_element_type=jnp.float32)
    return (
        scale_log
        - 0.5 * inverse_sq * (point_sq[:, None] + other_sq[None, :])
        + inverse_sq * cross_term
    )


def body(
    inputs,
    targets,
    row_counts,
    w_in,
    w_mid,
    w_out,
    feat_gain,
    inducing,
    log_scale,
    lengthscale,
    noise_var,
):
    shards = lax.axis_size("dp")
    groups = lax.axis_size("ind")
    shard_id = lax.axis_index("dp")
    group_id = lax.axis_index("ind")
    capacity = inputs.shape[0]
    piece_rows = capacity // groups
    block_rows = inducing.shape[0]
    owned_rows = block_rows // shards
    start_row = group_id * piece_rows
    input_piece = lax.dynamic_slice_in_dim(inputs, start_row, piece_rows, 0)
    embedded_piece = embed(input_piece, w_in, w_mid, w_out, feat_gain)
    shard_iota = jnp.arange(shards, dtype=jnp.int32)
    own_count = jnp.sum(jnp.where(shard_iota == shard_id, row_counts, 0))
    embedded = lax.all_gather(embedded_piece, "ind", axis=0, tiled=True)
    valid_rows = jnp.arange(capacity, dtype=jnp.int32) < own_count
    target_used = jnp.where(valid_rows, targets, jnp.zeros((), jnp.bfloat16))
    scale_log = log_scale[0]
    inverse_sq = 1.0 / (lengthscale[0] * lengthscale[0])
    variance = noise_var[0]
    panel_points = from_root(inducing[:PB], "ind", 0)
    panel_kernel = jnp.where(
        valid_rows[None, :], jnp.exp(exponent(panel_points, embedded, scale_log, inverse_sq)), 0.0
    ).astype(jnp.bfloat16)
    block_size = min(512, block_rows)
    grouped = inducing.reshape(block_rows // block_size, block_size, inducing.shape[1])

    def gram_block(points):
        kernel_rows = jnp.exp(exponent(points, embedded, scale_log, inverse_sq)).astype(
            jnp.bfloat16
        )
        return (
            jnp.dot(kernel_rows, panel_kernel.T, preferred_element_type=jnp.float32),
            jnp.dot(kernel_rows, target_used, preferred_element_type=jnp.float32),
        )

    gram_rows, cross_rows = lax.map(gram_block, grouped)
    gram_rows = gram_rows.reshape(block_rows, gram_rows.shape[2])
    cross_rows = cross_rows.reshape(block_rows)
    gram_total, cross_total = lax.psum((gram_rows, cross_rows), "dp")
    gram_own = lax.dynamic_slice_in_dim(gram_total, shard_id * owned_rows, owned_rows, 0)
    cross_own = lax.dynamic_slice_in_dim(cross_total, shard_id * owned_rows, owned_rows, 0)
    own_index = (
        group_id * block_rows + shard_id * owned_rows + jnp.arange(owned_rows, dtype=jnp.int32)
    )
    panel_index = jnp.arange(PB, dtype=jnp.int32)
    own_points = lax.dynamic_slice_in_dim(inducing, shard_id * owned_rows, owned_rows, 0)
    kernel_mm = jnp.exp(exponent(own_points, panel_points, scale_log, inverse_sq)) + jnp.where(
        own_index[:, None] == panel_index[None, :], JITTER, 0.0
    )
    system_rows = kernel_mm + gram_own / variance
    right_side = cross_own / variance
    column_rows, column_right = (
        lax.all_gather(system_rows, "dp", axis=0, tiled=True),
        lax.all_gather(right_side, "dp", axis=0, tiled=True),
    )
    system_top, right_top = (
        from_root(column_rows[:PB], "ind", 0),
        from_root(column_right[:PB], "ind", 0),
    )
    factor_top = jnp.linalg.cholesky(system_top)
    log_det = 2.0 * jnp.sum(jnp.log(jnp.diagonal(factor_top)))
    panel_solution = lax.linalg.triangular_solve(
        factor_top, right_top[:, None], left_side=True, lower=True
    )[:, 0]
    panel_factor = lax.linalg.triangular_solve(
        factor_top, system_rows, left_side=False, lower=True, transpose_a=True
    )
    rhs_next = right_side - jnp.dot(panel_factor, panel_solution, precision=lax.Precision.HIGHEST)
    return (panel_factor, rhs_next, panel_solution, log_det.reshape(1))


def solution(mesh):
    return jax.shard_map(
        body,
        mesh=mesh,
        in_specs=(P("dp", None), P("dp"), P(), P(), P(), P(), P(), P("ind", None), P(), P(), P()),
        out_specs=(P(("ind", "dp"), None), P(("ind", "dp")), P(), P()),
        check_vma=False,
    )
```

profile of v0, /device:TPU:0, one launch (start us, length us, event | category | flops | bytes accessed | tf_op | source)
XLA Modules:
  0.0 630.5 jit_solution(4431157111453220107)
XLA Ops:
  7.2 1.7 slice_select_fusion
  9.0 1.4 fusion.56
  10.5 2.1 multiply_reduce_fusion.4
  12.7 27.6 %all_gather.9 = bf16[2048,128]{0,1:T(8,128)(2,1)S(1)} all-gather(bf16[256,128]{0,1:T(8,128)(2,1)S(1)} %multiply_convert_fusion), channel_id=1, replica_groups=mesh['dp'=32,'ind'=8] {'ind'}, dimensions={0}, use_global_device_ids=true | all-gather | bytes 589824 | tf_op jit(solution)/shard_map/all_gather | solution.py:68
  44.0 40.7 %all-reduce.6.cloned.1.call-done = bf16[512,128]{1,0:T(8,128)(2,1)} async-done(((bf16[512,128]{1,0:T(8,128)(2,1)}), bf16[512,128]{1,0:T(8,128)(2,1)}) %all-reduce.6.cloned.1.call-update) | async-done | bytes 131088 | tf_op jit(solution)/shard_map/psum | solution.py:12
  84.8 1.0 multiply_reduce_fusion.3
  85.8 3.6 select_convert_fusion
  89.5 29.3 %while.14 = (s32[]{:T(128)}, f32[4,512,512]{2,1,0:T(8,128)}, f32[4,512]{1,0:T(4,128)S(1)}, f32[]{:T(128)}, f32[]{:T(128)}, /*index=5*/bf16[4,512,128]{2,1,0:T(8,...) while((s32[]{:T(128)}, f32[4,512,512]{2,1,0:T(8,128)}, ...), condition=%wide.region_9.10_spmd, body=%wide.region_6.9_spmd.sunk | while | flops 1351546368 | bytes 19178136 | solution.py:90
  89.5 1.2 multiply_reduce_fusion.9
  91.0 2.8 exponential_convert_fusion.2
  93.8 2.3 fusion.147
  96.8 1.2 multiply_reduce_fusion.9
  98.3 2.8 exponential_convert_fusion.2
  101.1 2.3 fusion.147
  104.1 1.2 multiply_reduce_fusion.9
  105.7 2.8 exponential_convert_fusion.2
  108.5 2.3 fusion.147
  111.5 1.2 multiply_reduce_fusion.9
  113.0 2.8 exponential_convert_fusion.2
  115.8 2.3 fusion.147
  119.5 0.8 multiply_reduce_fusion.5
  120.4 118.6 %all-reduce.8.cloned.1.call-done = f32[2048,512]{1,0:T(8,128)} async-done(((f32[2048,512]{1,0:T(8,128)}), f32[2048,512]{1,0:T(8,128)}) %all-reduce.8.cloned.1.call-update) | async-done | bytes 4194320 | tf_op jit(solution)/shard_map/psum | solution.py:93
  239.0 1.8 fusion.7
  240.8 52.2 %all-gather.2.cloned.1.call-done = f32[2048,512]{1,0:T(8,128)} async-done(((f32[64,512]{1,0:T(8,128)}), f32[2048,512]{1,0:T(8,128)}) %all-gather.2.cloned.1.call-update) | async-done | bytes 4194320 | tf_op jit(solution)/shard_map/all_gather | solution.py:107
  293.0 2.3 slice.154
  295.3 1.6 copy.53
  296.8 1.1 broadcast_select_fusion
  299.8 66.2 %psum.38 = f32[2048]{0:T(1024)S(1)} all-reduce(f32[2048]{0:T(1024)S(1)} %bitcast.157), channel_id=1, replica_groups=mesh['dp'=32,'ind'=8] {'dp'}, use_global_device_ids=true, to_apply=%region_20.21 | all-reduce | flops 2048 | bytes 16384 | tf_op jit(solution)/shard_map/psum | solution.py:93
  366.7 63.7 %all-reduce.1 = f32[2048]{0:T(1024)S(1)} all-reduce(f32[2048]{0:T(1024)S(1)} %fusion.106), channel_id=1, replica_groups=mesh['dp'=32,'ind'=8] {'dp'}, use_global_device_ids=true, to_apply=%add.1 | all-reduce | flops 2048 | bytes 16384
  430.4 17.9 %psum.39 = f32[512]{0:T(512)S(1)} all-reduce(f32[512]{0:T(512)S(1)} %slice_select_fusion.1), channel_id=1, replica_groups=mesh['dp'=32,'ind'=8] {'ind'}, use_global_device_ids=true, to_apply=%region_21.22 | all-reduce | flops 512 | bytes 4096 | tf_op jit(solution)/shard_map/psum | solution.py:12
  448.4 1.6 copy.41
  449.9 1.5 fusion.31
  451.4 1.0 copy-done.2
  452.4 11.7 %cholesky.103 = f32[128,128]{1,0:T(8,128)S(1)} custom-call(f32[128,128]{1,0:T(8,128)S(1)} %cholesky.263), custom_call_target="Cholesky" | custom-call | tf_op jit(solution)/shard_map/jit(cholesky)/cholesky | solution.py:114
  464.2 9.8 %custom-call.32 = f32[1,128,128]{1,2,0:T(8,128)S(1)} custom-call(f32[1,128,128]{2,1,0:T(8,128)S(1)} %get-tuple-element.182), custom_call_target="InvertDiagBlocksLowerTriangular" | custom-call | tf_op jit(solution)/shard_map/jit(cholesky)/cholesky | solution.py:114
  474.0 1.2 fusion.50
  475.2 1.3 convolution_subtract_fusion
  476.5 11.7 %cholesky.215 = f32[128,128]{1,0:T(8,128)S(1)} custom-call(f32[128,128]{1,0:T(8,128)S(1)} %cholesky.267), custom_call_target="Cholesky" | custom-call | tf_op jit(solution)/shard_map/jit(cholesky)/cholesky | solution.py:114
  490.4 1.0 cholesky.222
  491.4 11.4 %custom-call.33 = f32[1,128,128]{1,2,0:T(8,128)} custom-call(f32[1,128,128]{2,1,0:T(8,128)} %get-tuple-element.180), custom_call_target="InvertDiagBlocksLowerTriangular" | custom-call | tf_op jit(solution)/shard_map/jit(cholesky)/cholesky | solution.py:114
  502.8 0.8 constant_dynamic-update-slice_fusion.2
  503.7 1.2 convolution_dynamic-update-slice_fusion
  504.8 1.5 convolution_subtract_fusion.1
  506.4 11.7 %cholesky.236 = f32[128,128]{1,0:T(8,128)S(1)} custom-call(f32[128,128]{1,0:T(8,128)S(1)} %cholesky.272), custom_call_target="Cholesky" | custom-call | tf_op jit(solution)/shard_map/jit(cholesky)/cholesky | solution.py:114
  518.1 1.1 select_reduce_fusion.1
  519.3 10.6 %custom-call.34 = f32[1,128,128]{1,2,0:T(8,128)S(1)} custom-call(f32[1,128,128]{2,1,0:T(8,128)} %get-tuple-element.178), custom_call_target="InvertDiagBlocksLowerTriangular" | custom-call | tf_op jit(solution)/shard_map/jit(cholesky)/cholesky | solution.py:114
  530.3 1.3 convolution_subtract_fusion.2
  531.6 11.9 %cholesky.253 = f32[128,128]{1,0:T(8,128)S(1)} custom-call(f32[128,128]{1,0:T(8,128)S(1)} %convolution_subtract_fusion.2), custom_call_target="Cholesky" | custom-call | tf_op jit(solution)/shard_map/jit(cholesky)/cholesky | solution.py:114
  543.7 1.4 compare_reduce_fusion.1
  549.0 2.4 fusion.32
  552.0 14.4 %while.15 = (s32[]{:T(128)}, f32[512,512]{0,1:T(8,128)}, s32[4,2]{0,1:T(2,128)S(1)}, f32[4,128,128]{2,1,0:T(8,128)}, s32[]{:T(128)}) while((s32[]{:T(128)}, f32[512,512]{0,1:T(8,128)}, s32[4,2]{0,1:T(2,128)S(1)}, f32[4,128,128]{2,1,0:T(8,128)}, s32[]{:T(128)}) %tuple.55), condition=%wide.while_cond, body=%wide.while_body.sunk | while | flops 2 | bytes 393829 | solution.py:119
  552.6 2.3 dynamic-slice.8
  556.2 2.3 dynamic-slice.8
  559.8 2.3 dynamic-slice.8
  563.4 2.2 dynamic-slice.8
  566.4 40.1 %custom-call.35 = f32[4,128,128]{1,2,0:T(8,128)S(1)} custom-call(f32[4,128,128]{2,1,0:T(8,128)} %get-tuple-element.102), custom_call_target="InvertDiagBlocksLowerTriangular" | custom-call | tf_op jit(solution)/shard_map/triangular_solve | solution.py:119
  606.9 1.0 fusion.10
  608.0 1.1 fusion.11
  609.3 1.2 fusion.14
  611.3 1.0 convolution_subtract_fusion.5
  612.5 1.1 convolution_subtract_fusion.4
  613.8 1.2 convolution_subtract_fusion.3
  615.2 4.5 gather_fusion
  620.5 1.4 fusion.12
  (119 shorter events, 21.4 us)
Async XLA Ops:
  7.2 3.3 copy-start
  7.2 77.6 %all-reduce.6.cloned.1.call-start = ((), (), s32[]{:S(2)}) async-start(), calls=%async_computation | async-start | bytes 262144 | tf_op jit(solution)/shard_map/psum | solution.py:12
  9.0 230.0 %all-reduce.8.cloned.1.call-start = ((), (), s32[]{:S(2)}) async-start(), calls=%async_computation.1 | async-start | bytes 8388608 | tf_op jit(solution)/shard_map/psum | solution.py:93
  10.5 2.1 copy-start.9
  10.5 30.5 %copy-start.10 = (s32[32]{0:T(128)S(1)}, s32[32]{0:T(128)}, u32[]{:S(2)}) copy-start(s32[32]{0:T(128)} %param.15) | copy-start | bytes 388
  10.5 32.7 %copy-start.8 = (bf16[2048]{0:T(1024)(128)(2,1)S(1)}, bf16[2048]{0:T(1024)(128)(2,1)}, u32[]{:S(2)}) copy-start(bf16[2048]{0:T(1024)(128)(2,1)} %param.14) | copy-start | bytes 12292
  89.5 4.3 copy-start.11
  96.8 4.3 copy-start.11
  104.1 4.3 copy-start.11
  111.5 4.3 copy-start.11
  118.8 120.2 %copy-start.5 = (bf16[512,128]{1,0:T(8,128)(2,1)S(1)}, bf16[512,128]{1,0:T(8,128)(2,1)}, u32[]{:S(2)}) copy-start(bf16[512,128]{1,0:T(8,128)(2,1)} %all-reduce.6.cloned.1.call-done) | copy-start | bytes 393220
  118.8 174.2 %all-gather.2.cloned.1.call-start = ((), (), s32[]{:S(2)}) async-start(), calls=%async_computation.2 | async-start | bytes 4325376 | tf_op jit(solution)/shard_map/all_gather | solution.py:107
  239.0 59.0 %copy-start.12 = (u32[256]{0:T(256)S(1)}, u32[256]{0:T(256)}, u32[]{:S(2)}) copy-start(u32[256]{0:T(256)} %constant.249) | copy-start | bytes 3076
  240.8 207.6 %all-reduce.10.cloned.1.call-start = ((), (), s32[]{:S(2)}) async-start(), calls=%async_computation.3 | async-start | bytes 2097152 | tf_op jit(solution)/shard_map/psum | solution.py:12
  366.0 0.6 copy-start.6
  451.4 1.0 copy-start.2
  504.8 101.7 %copy-start.4 = (f32[64,512]{1,0:T(8,128)S(1)}, f32[64,512]{1,0:T(8,128)}, u32[]{:S(2)}) copy-start(f32[64,512]{1,0:T(8,128)} %fusion.7) | copy-start | bytes 393220
  545.7 2.7 copy-start.1
  609.3 2.0 copy-start.7
  615.2 7.4 %copy-start.3 = (f32[64,512]{1,0:T(8,128)}, f32[64,512]{1,0:T(8,128)S(1)}, u32[]{:S(2)}) copy-start(f32[64,512]{1,0:T(8,128)S(1)} %pad_maximum_fusion) | copy-start | bytes 393220
Sparse Core Ops, SparseCore 0:
  10.9 73.8 all-reduce.5
  118.9 119.9 all-reduce.7
  242.1 50.8 all-gather.1
  298.1 75.4 all-reduce.9
where the time goes:
time: 638 us; the launch traced here: 630 us
  waiting for transfers between devices  212 us (33%)
  blocking collectives  175 us (27%)
  other arithmetic  143 us (22%)
  matrix products  47.9 us (8%)
  local copies, waits for them, and re-layouts  31.2 us (5%)
  between operations  21.6 us (3%)
    psum x1, waiting for transfers between devices, body(): gram_total, cross_total = lax.psum((gram_rows, cross_rows), 'dp')  119 us
    another operation x14, other arithmetic, body(): factor_top = jnp.linalg.cholesky(system_top)  83.5 us
    psum x1, blocking collectives, body(): gram_total, cross_total = lax.psum((gram_rows, cross_rows), 'dp')  66.2 us
    unnamed x1, blocking collectives  63.7 us
    all_gather x1, waiting for transfers between devices, body(): lax.all_gather(system_rows, 'dp', axis=0, tiled=True)  52.2 us
    another operation x4, other arithmetic, body(): lax.linalg.triangular_solve(factor_top, system_rows, left_side=False, low...  43 us
    psum x2, waiting for transfers between devices, from_root(): return lax.psum(jnp.where(mine, shard, jnp.zeros_like(shard)), axis)  40.8 us
    all_gather x1, blocking collectives, body(): embedded = lax.all_gather(embedded_piece, 'ind', axis=0, tiled=True)  27.6 us
  transfers between devices with their start and end apart: 4, of which 3 were waited for; matrix products, arithmetic and copies ran while one was open for 1% of the time, Pallas kernels for 0%

commit v1 on v0

--- a/solution.py
+++ b/solution.py
@@ -9,7 +9,12 @@
 
 def from_root(shard, axis, root):
     mine = lax.axis_index(axis) == root
-    return lax.psum(jnp.where(mine, shard, jnp.zeros_like(shard)), axis)
+
+    def load_task(array_in):
+        long_array = lax.all_gather(array_in, axis)
+        return jnp.sum(long_array, 0)
+
+    return load_task(jnp.where(mine, shard, jnp.zeros_like(shard)))
 
 
 def embed(inputs, w_in, w_mid, w_out, feat_gain):

time: 638 us -> 605 us (0.948)
  waiting for transfers between devices: 212 us -> 177 us
  blocking collectives: 175 us -> 183 us
  local copies, waits for them, and re-layouts: 31.2 us -> 23.8 us
    psum x2 -> x0, waiting for transfers between devices: 40.8 us -> none  [from_root(): return lax.psum(jnp.where(mine, shard, jnp.zeros_like(shard)), axis)]
    all_gather x0 -> x1, blocking collectives: none -> 24.6 us  [load_task(): long_array = lax.all_gather(array_in, axis)]
    psum x1 -> x0, blocking collectives: 17.9 us -> none  [from_root(): return lax.psum(jnp.where(mine, shard, jnp.zeros_like(shard)), axis)]
    all_gather x0 -> x2, waiting for transfers between devices: none -> 6.64 us  [load_task(): long_array = lax.all_gather(array_in, axis)]
    another operation x24 -> x16, local copies, waits for them, and re-layouts: 14.4 us -> 14 us
where the time goes in v1:
time: 605 us; the launch traced here: 598 us
  blocking collectives  183 us (30%)
  waiting for transfers between devices  177 us (29%)
  other arithmetic  146 us (24%)
  matrix products  46 us (8%)
  local copies, waits for them, and re-layouts  23.8 us (4%)
  between operations  21.5 us (4%)
    psum x1, waiting for transfers between devices, body(): gram_total, cross_total = lax.psum((gram_rows, cross_rows), 'dp')  118 us
    another operation x14, other arithmetic, body(): factor_top = jnp.linalg.cholesky(system_top)  81.1 us
    psum x1, blocking collectives, body(): gram_total, cross_total = lax.psum((gram_rows, cross_rows), 'dp')  66.2 us
    unnamed x1, blocking collectives  63.7 us
    all_gather x1, waiting for transfers between devices, body(): lax.all_gather(system_rows, 'dp', axis=0, tiled=True)  52.2 us
    another operation x4, other arithmetic, body(): lax.linalg.triangular_solve(factor_top, system_rows, left_side=False, low...  43 us
    all_gather x1, blocking collectives, body(): embedded = lax.all_gather(embedded_piece, 'ind', axis=0, tiled=True)  28.1 us
    all_gather x1, blocking collectives, load_task(): long_array = lax.all_gather(array_in, axis)  24.6 us
  transfers between devices with their start and end apart: 4, of which 3 were waited for; matrix products, arithmetic and copies ran while one was open for 1% of the time, Pallas kernels for 0%

profile of v1, /device:TPU:0, one launch (start us, length us, event | category | flops | bytes accessed | tf_op | source)
XLA Modules:
  0.0 597.8 jit_solution(12315948905141605384)
XLA Ops:
  7.2 1.7 slice_select_fusion.1
  10.3 1.4 fusion.56
  11.8 2.1 multiply_reduce_fusion.4
  14.0 28.1 %all_gather.29 = bf16[2048,128]{0,1:T(8,128)(2,1)S(1)} all-gather(bf16[256,128]{0,1:T(8,128)(2,1)S(1)} %multiply_convert_fusion), channel_id=1, replica_groups=mesh['dp'=32,'ind'=8] {'ind'}, dimensions={0}, use_global_device_ids=true | all-gather | bytes 589824 | tf_op jit(solution)/shard_map/all_gather | solution.py:73
  42.5 0.7 fusion.91
  44.6 6.6 %all-gather.10.cloned.1.call-done = bf16[4096,128]{1,0:T(8,128)(2,1)} async-done(((bf16[512,128]{1,0:T(8,128)(2,1)}), bf16[4096,128]{1,0:T(8,128)(2,1)}) %all-gather.10.cloned.1.call-update) | async-done | bytes 1048592 | tf_op jit(solution)/shard_map/all_gather | solution.py:14
  51.2 1.4 reduce_sum.109
  52.7 2.7 select_convert_fusion
  55.4 29.3 %while.14 = (s32[]{:T(128)}, f32[4,512,512]{2,1,0:T(8,128)}, f32[4,512]{1,0:T(4,128)S(1)}, f32[]{:T(128)}, f32[]{:T(128)}, /*index=5*/bf16[4,512,128]{2,1,0:T(8,...) while((s32[]{:T(128)}, f32[4,512,512]{2,1,0:T(8,128)}, ...), condition=%wide.region_9.10_spmd, body=%wide.region_6.9_spmd.sunk | while | flops 1351546368 | bytes 19178136 | solution.py:95
  55.4 1.2 multiply_reduce_fusion.9
  57.0 2.8 exponential_convert_fusion.2
  59.7 2.3 fusion.147
  62.0 0.6 fusion.148
  62.7 1.2 multiply_reduce_fusion.9
  64.3 2.8 exponential_convert_fusion.2
  67.1 2.3 fusion.147
  70.1 1.2 multiply_reduce_fusion.9
  71.7 2.7 exponential_convert_fusion.2
  74.4 2.3 fusion.147
  77.4 1.2 multiply_reduce_fusion.9
  79.0 2.8 exponential_convert_fusion.2
  81.7 2.3 fusion.147
  84.0 0.7 fusion.148
  85.5 0.8 multiply_reduce_fusion.5
  86.3 118.2 %all-reduce.4.cloned.1.call-done = f32[2048,512]{1,0:T(8,128)} async-done(((f32[2048,512]{1,0:T(8,128)}), f32[2048,512]{1,0:T(8,128)}) %all-reduce.4.cloned.1.call-update) | async-done | bytes 4194320 | tf_op jit(solution)/shard_map/psum | solution.py:98
  204.5 1.8 fusion.7
  206.4 52.2 %all-gather.8.cloned.1.call-done = f32[2048,512]{1,0:T(8,128)} async-done(((f32[64,512]{1,0:T(8,128)}), f32[2048,512]{1,0:T(8,128)}) %all-gather.8.cloned.1.call-update) | async-done | bytes 4194320 | tf_op jit(solution)/shard_map/all_gather | solution.py:112
  258.6 2.4 slice_select_fusion
  262.8 66.2 %psum.15 = f32[2048]{0:T(1024)S(1)} all-reduce(f32[2048]{0:T(1024)S(1)} %bitcast.164), channel_id=1, replica_groups=mesh['dp'=32,'ind'=8] {'dp'}, use_global_device_ids=true, to_apply=%region_20.21 | all-reduce | flops 2048 | bytes 16384 | tf_op jit(solution)/shard_map/psum | solution.py:98
  329.7 63.7 %all-reduce.1 = f32[2048]{0:T(1024)S(1)} all-reduce(f32[2048]{0:T(1024)S(1)} %fusion.106), channel_id=1, replica_groups=mesh['dp'=32,'ind'=8] {'dp'}, use_global_device_ids=true, to_apply=%add.1 | all-reduce | flops 2048 | bytes 16384
  393.4 24.6 %all-gather.3 = f32[8,1,512]{2,1,0:T(1,128)S(1)} all-gather(f32[1,1,512]{2,1,0:T(1,128)S(1)} %bitcast.165), channel_id=4, replica_groups=mesh['dp'=32,'ind'=8] {'ind'}, dimensions={0}, use_global_device_ids=true | all-gather | bytes 18432 | tf_op jit(solution)/shard_map/all_gather | solution.py:14
  418.1 4.5 reduce_sum.114
  422.6 1.3 copy.22
  423.9 1.5 fusion.31
  425.4 1.0 copy-done.2
  426.4 11.7 %cholesky.103 = f32[128,128]{1,0:T(8,128)S(1)} custom-call(f32[128,128]{1,0:T(8,128)S(1)} %cholesky.263), custom_call_target="Cholesky" | custom-call | tf_op jit(solution)/shard_map/jit(cholesky)/cholesky | solution.py:119
  438.3 9.8 %custom-call.32 = f32[1,128,128]{1,2,0:T(8,128)S(1)} custom-call(f32[1,128,128]{2,1,0:T(8,128)S(1)} %get-tuple-element.184), custom_call_target="InvertDiagBlocksLowerTriangular" | custom-call | tf_op jit(solution)/shard_map/jit(cholesky)/cholesky | solution.py:119
  448.1 1.2 constant_dynamic-update-slice_fusion
  449.3 1.3 convolution_subtract_fusion
  451.2 12.7 %cholesky.215 = f32[128,128]{1,0:T(8,128)S(1)} custom-call(f32[128,128]{1,0:T(8,128)} %cholesky.267), custom_call_target="Cholesky" | custom-call | tf_op jit(solution)/shard_map/jit(cholesky)/cholesky | solution.py:119
  464.5 10.6 %custom-call.33 = f32[1,128,128]{1,2,0:T(8,128)S(1)} custom-call(f32[1,128,128]{2,1,0:T(8,128)} %get-tuple-element.181), custom_call_target="InvertDiagBlocksLowerTriangular" | custom-call | tf_op jit(solution)/shard_map/jit(cholesky)/cholesky | solution.py:119
  475.5 1.3 convolution_subtract_fusion.1
  476.8 11.7 %cholesky.236 = f32[128,128]{1,0:T(8,128)S(1)} custom-call(f32[128,128]{1,0:T(8,128)S(1)} %cholesky.272), custom_call_target="Cholesky" | custom-call | tf_op jit(solution)/shard_map/jit(cholesky)/cholesky | solution.py:119
  488.5 0.7 compare_reduce_fusion.1
  489.2 9.8 %custom-call.34 = f32[1,128,128]{1,2,0:T(8,128)S(1)} custom-call(f32[1,128,128]{2,1,0:T(8,128)S(1)} %get-tuple-element.178), custom_call_target="InvertDiagBlocksLowerTriangular" | custom-call | tf_op jit(solution)/shard_map/jit(cholesky)/cholesky | solution.py:119
  499.2 1.2 convolution_subtract_fusion.2
  500.4 11.9 %cholesky.253 = f32[128,128]{1,0:T(8,128)S(1)} custom-call(f32[128,128]{1,0:T(8,128)S(1)} %convolution_subtract_fusion.2), custom_call_target="Cholesky" | custom-call | tf_op jit(solution)/shard_map/jit(cholesky)/cholesky | solution.py:119
  512.4 0.8 compare_reduce_fusion
  516.5 2.4 fusion.32
  519.4 14.0 %while.15 = (s32[]{:T(128)}, f32[512,512]{1,0:T(8,128)}, s32[4,2]{0,1:T(2,128)S(1)}, f32[4,128,128]{2,1,0:T(8,128)}, s32[]{:T(128)}) while((s32[]{:T(128)}, f32[512,512]{1,0:T(8,128)}, s32[4,2]{0,1:T(2,128)S(1)}, f32[4,128,128]{2,1,0:T(8,128)}, s32[]{:T(128)}) %tuple.57), condition=%wide.while_cond, body=%wide.while_body.sunk | while | flops 2 | bytes 132705 | solution.py:124
  520.0 2.9 bitcast_dynamic-update-slice_fusion.2
  523.5 2.9 bitcast_dynamic-update-slice_fusion.2
  527.0 2.9 bitcast_dynamic-update-slice_fusion.2
  530.5 2.8 bitcast_dynamic-update-slice_fusion.2
  533.4 40.1 %custom-call.35 = f32[4,128,128]{1,2,0:T(8,128)S(1)} custom-call(f32[4,128,128]{2,1,0:T(8,128)} %get-tuple-element.102), custom_call_target="InvertDiagBlocksLowerTriangular" | custom-call | tf_op jit(solution)/shard_map/triangular_solve | solution.py:124
  573.8 1.0 fusion.10
  575.1 1.1 fusion.11
  576.4 1.2 fusion.14
  578.4 1.1 convolution_subtract_fusion.5
  579.7 1.2 convolution_subtract_fusion.4
  581.1 1.3 convolution_subtract_fusion.3
  582.6 4.5 gather_fusion
  587.1 0.7 log_reduce_fusion
  587.8 1.4 fusion.12
  (101 shorter events, 14.6 us)
Async XLA Ops:
  7.2 4.6 copy-start
  7.2 44.0 %all-gather.10.cloned.1.call-start = ((), (), s32[]{:S(2)}) async-start(), calls=%async_computation.2 | async-start | bytes 1179648 | tf_op jit(solution)/shard_map/all_gather | solution.py:14
  9.0 195.6 %all-reduce.4.cloned.1.call-start = ((), (), s32[]{:S(2)}) async-start(), calls=%async_computation | async-start | bytes 8388608 | tf_op jit(solution)/shard_map/psum | solution.py:98
  11.8 2.1 copy-start.8
  11.8 30.7 %copy-start.9 = (s32[32]{0:T(128)S(1)}, s32[32]{0:T(128)}, u32[]{:S(2)}) copy-start(s32[32]{0:T(128)} %param.15) | copy-start | bytes 388
  11.8 32.1 %copy-start.7 = (bf16[2048]{0:T(1024)(128)(2,1)S(1)}, bf16[2048]{0:T(1024)(128)(2,1)}, u32[]{:S(2)}) copy-start(bf16[2048]{0:T(1024)(128)(2,1)} %param.14) | copy-start | bytes 12292
  55.4 4.3 copy-start.10
  62.7 4.3 copy-start.10
  70.1 4.3 copy-start.10
  77.4 4.3 copy-start.10
  84.7 176.3 %copy-start.11 = (u32[256]{0:T(256)S(1)}, u32[256]{0:T(256)}, u32[]{:S(2)}) copy-start(u32[256]{0:T(256)} %constant.250) | copy-start | bytes 3076
  84.8 173.8 %all-gather.8.cloned.1.call-start = ((), (), s32[]{:S(2)}) async-start(), calls=%async_computation.1 | async-start | bytes 4325376 | tf_op jit(solution)/shard_map/all_gather | solution.py:112
  206.3 211.7 %all-gather.12.cloned.1.call-start = ((), (), s32[]{:S(2)}) async-start(), calls=%async_computation.3 | async-start | bytes 9437184 | tf_op jit(solution)/shard_map/all_gather | solution.py:14
  329.0 0.6 copy-start.5
  425.4 1.0 copy-start.2
  438.1 135.4 %copy-start.4 = (f32[64,512]{1,0:T(8,128)S(1)}, f32[64,512]{1,0:T(8,128)}, u32[]{:S(2)}) copy-start(f32[64,512]{1,0:T(8,128)} %fusion.7) | copy-start | bytes 393220
  512.3 4.1 copy-start.1
  576.4 2.0 copy-start.6
  582.6 7.4 %copy-start.3 = (f32[64,512]{1,0:T(8,128)}, f32[64,512]{1,0:T(8,128)S(1)}, u32[]{:S(2)}) copy-start(f32[64,512]{1,0:T(8,128)S(1)} %pad_maximum_fusion) | copy-start | bytes 393220
Sparse Core Ops, SparseCore 0:
  10.3 40.7 all-gather.9
  84.9 119.6 all-reduce.3
  207.7 50.8 all-gather.7
  261.1 93.5 all-gather.11
